TPU v7x, 32 devices: a whole 2x2x4 slice. The times are simulated.
32 devices in a mesh: shard: 8 (over y, x, core), rep: 4 (over z).
Axes of the slice: x: 2, y: 2, z: 4, core: 2. Of those that a mesh axis runs over, the one named last changes fastest.
Arguments:
- inputs: float32 [8192, 768], P(('shard', 'rep')), may hold values from -6 to 6
- image_ids: int32 [8192], P(('shard', 'rep')), may hold values from 0 to 50, never falling along the last dimension, each value on 1 to 197 neighbouring positions
- output_gradient: float32 [8192, 768], P(('shard', 'rep')), may hold values from -6 to 6
- first_norm_scale: float32 [768], P('shard'), may hold values from 0.5 to 1.5
- first_norm_bias: float32 [768], P('shard'), may hold values from -1.5 to 1.5
- w_qkv: float32 [768, 2304], P('shard'), may hold values from -0.45 to 0.45
- bias_query: float32 [768], P('shard'), may hold values from -1.5 to 1.5
- bias_value: float32 [768], P('shard'), may hold values from -1.5 to 1.5
- w_output: float32 [768, 768], P('shard'), may hold values from -1.75 to 1.75
- bias_output: float32 [768], P('shard'), may hold values from -1.5 to 1.5
- second_norm_scale: float32 [768], P('shard'), may hold values from 0.5 to 1.5
- second_norm_bias: float32 [768], P('shard'), may hold values from -1.5 to 1.5
- w_up: float32 [768, 3072], P('shard'), may hold values from -0.21875 to 0.21875
- bias_up: float32 [3072], P('shard'), may hold values from -1.5 to 1.5
- w_down: float32 [3072, 768], P(None, 'shard'), may hold values from -0.109375 to 0.109375
- bias_down: float32 [768], P('shard'), may hold values from -1.5 to 1.5
Outputs:
- outputs: float32 [8192, 768], P(('shard', 'rep'))
- gradient_of_input: float32 [8192, 768], P(('shard', 'rep'))
- gradient_first_norm_scale: float32 [768], P('shard')
- grad_norm1_bias: float32 [768], P('shard')
- grad_w_qkv: float32 [768, 2304], P('shard')
- grad_bias_query: float32 [768], P('shard')
- grad_bias_value: float32 [768], P('shard')
- grad_w_output: float32 [768, 768], P('shard')
- grad_bias_output: float32 [768], P('shard')
- gradient_second_norm_scale: float32 [768], P('shard')
- grad_norm2_bias: float32 [768], P('shard')
- grad_w_up: float32 [768, 3072], P('shard')
- grad_bias_up: float32 [3072], P('shard')
- grad_w_down: float32 [3072, 768], P(None, 'shard')
- grad_bias_down: float32 [768], P('shard')
Inputs may be any that keep to these rules, and one draw needn't show every extreme that they name: `image_ids`: image ids never fall from one slot to the next; each image holds 1 to 197 consecutive slots, and some image exactly 197.
All inputs are finite; a program needn't handle non-finite values.
Results may differ from a plain program's by a relative error of at most 0.0003.
Values sent between devices are 32-bit elements; how exact they have to be, the bound alone decides.
No kernel may reach another device: no remote copies, remote signals or barrier semaphores. Data moves between devices by JAX's collectives and lax.ppermute only.
A program may use at most 192 MiB of HBM per device.

v0:
```python
import math

import jax
import jax.numpy as jnp
from jax import lax
from jax.experimental import pallas as pl
from jax.experimental.pallas import tpu as pltpu
from jax.sharding import PartitionSpec as P


HEAD = 64
REACH = 200
PAD = 8
HIGH = lax.Precision.HIGH
EXACT = lax.Precision.HIGHEST


def matmul(left, right, dims=((1,), (0,))):
    return lax.dot_general(
        left, right, (dims, ((), ())), precision=HIGH, preferred_element_type=jnp.float32
    )


def layer_norm_forward(rows, norm_scale, norm_bias):
    centered_input = rows - jnp.mean(rows, axis=-1, keepdims=True)
    inverse_deviation = lax.rsqrt(
        jnp.mean(centered_input * centered_input, axis=-1, keepdims=True) + 1e-06
    )
    standardized = centered_input * inverse_deviation
    return (standardized * norm_scale + norm_bias, standardized, inverse_deviation)


def layer_norm_backward(upstream_gradient, standardized, inverse_deviation, norm_scale):
    scaled_values = upstream_gradient * norm_scale
    return inverse_deviation * (
        scaled_values
        - jnp.mean(scaled_values, axis=-1, keepdims=True)
        - standardized * jnp.mean(scaled_values * standardized, axis=-1, keepdims=True)
    )


def gelu_parts(pre):
    cdf = 0.5 * (1.0 + jax.scipy.special.erf(pre / math.sqrt(2.0)))
    slope = cdf + pre * jnp.exp(-0.5 * pre * pre) / math.sqrt(2.0 * math.pi)
    return (pre * cdf, slope)


def halves(x):
    hi = x.astype(jnp.bfloat16)
    lo = (x - hi.astype(jnp.float32)).astype(jnp.bfloat16)
    return hi, lo


def left3(x):
    hi, lo = halves(x)
    return jnp.concatenate([hi, hi, lo], axis=1)


def right3(x):
    hi, lo = halves(x)
    return jnp.concatenate([hi, lo, hi], axis=1)


def dot_nt(a, b):
    return lax.dot_general(a, b, (((1,), (1,)), ((), ())), preferred_element_type=jnp.float32)


def weighted(p, x):
    hi, lo = halves(p)
    xh, xl = halves(x)
    both = jnp.dot(hi, jnp.concatenate([xh, xl], axis=1), preferred_element_type=jnp.float32)
    return both[:, :HEAD] + both[:, HEAD:] + jnp.dot(lo, xh, preferred_element_type=jnp.float32)


def forward_kernel(q_ref, k_ref, v_ref, idc_ref, idr_ref, out_ref, lse_ref):
    same = idc_ref[0] == idr_ref[0]
    outs, lses = [], []
    for h in range(2):
        cols = slice(h * HEAD, (h + 1) * HEAD)
        q = q_ref[0][:, cols] * (1.0 / math.sqrt(HEAD))
        s = dot_nt(left3(q), right3(k_ref[0][:, cols]))
        s = jnp.where(same, s, -1e30)
        top = jnp.max(s, axis=1, keepdims=True)
        w = jnp.exp(s - top)
        total = jnp.sum(w, axis=1, keepdims=True)
        outs.append(weighted(w, v_ref[0][:, cols]) / total)
        lses.append(jnp.broadcast_to(top + jnp.log(total), (q.shape[0], HEAD)))
    out_ref[0] = jnp.concatenate(outs, axis=1)
    lse_ref[0] = jnp.concatenate(lses, axis=1)


def query_kernel(q_ref, k_ref, v_ref, g_ref, out_ref, lse_ref, idc_ref, idr_ref, dq_ref):
    same = idc_ref[0] == idr_ref[0]
    scale = 1.0 / math.sqrt(HEAD)
    outs = []
    for h in range(2):
        cols = slice(h * HEAD, (h + 1) * HEAD)
        q, k = q_ref[0][:, cols] * scale, k_ref[0][:, cols]
        g = g_ref[0][:, cols]
        lse = lse_ref[0][:, h * HEAD : h * HEAD + 1]
        delta = jnp.sum(g * out_ref[0][:, cols], axis=1, keepdims=True)
        s = dot_nt(left3(q), right3(k))
        p = jnp.exp(jnp.where(same, s - lse, -1e30))
        d_p = dot_nt(left3(g), right3(v_ref[0][:, cols]))
        outs.append(weighted(p * (d_p - delta), k) * scale)
    dq_ref[0] = jnp.concatenate(outs, axis=1)


def key_kernel(q_ref, g_ref, lse_ref, delta_ref, k_ref, v_ref, idc_ref, idr_ref, dk_ref, dv_ref):
    same = idc_ref[0] == idr_ref[0]
    scale = 1.0 / math.sqrt(HEAD)
    d_k, d_v = [], []
    for h in range(2):
        cols = slice(h * HEAD, (h + 1) * HEAD)
        q = q_ref[0][:, cols] * scale
        g = g_ref[0][:, cols]
        row = 2 * pl.program_id(1) + h
        lse = lse_ref[0, pl.ds(row, 1), :]
        delta = delta_ref[0, pl.ds(row, 1), :]
        s = dot_nt(left3(k_ref[0][:, cols]), right3(q))
        p = jnp.exp(jnp.where(same, s - lse, -1e30))
        d_p = dot_nt(left3(v_ref[0][:, cols]), right3(g))
        d_v.append(weighted(p, g))
        d_k.append(weighted(p * (d_p - delta), q))
    dk_ref[0] = jnp.concatenate(d_k, axis=1)
    dv_ref[0] = jnp.concatenate(d_v, axis=1)


def head_block(rows, first=0):
    return pl.BlockSpec((1, rows, 2 * HEAD), lambda b, h: (b, 0, first + h))


def whole_block(*shape):
    return pl.BlockSpec((1,) + shape, lambda b, h: (b, 0, 0))


def attention_forward(proj, ids_col, ids_row, own, width):
    blocks, ext, _ = proj.shape
    pairs = width // (2 * HEAD)
    return pl.pallas_call(
        forward_kernel,
        grid=(blocks, pairs),
        in_specs=[
            head_block(own),
            head_block(ext, pairs),
            head_block(ext, 2 * pairs),
            whole_block(own, 1),
            whole_block(1, ext),
        ],
        out_specs=[head_block(own), head_block(own)],
        out_shape=[jax.ShapeDtypeStruct((blocks, own, width), jnp.float32)] * 2,
        name="attend",
    )(proj, proj, proj, ids_col, ids_row)


def attention_queries(proj, grads, out, lse, ids_col, ids_row, own, width):
    blocks, ext, _ = proj.shape
    pairs = width // (2 * HEAD)
    return pl.pallas_call(
        query_kernel,
        grid=(blocks, pairs),
        in_specs=[
            head_block(own),
            head_block(ext, pairs),
            head_block(ext, 2 * pairs),
            head_block(own),
            head_block(own),
            head_block(own),
            whole_block(own, 1),
            whole_block(1, ext),
        ],
        out_specs=head_block(own),
        out_shape=jax.ShapeDtypeStruct((blocks, own, width), jnp.float32),
        name="grad_queries",
    )(proj, proj, proj, grads, out, lse, ids_col, ids_row)


def attention_keys(proj, grads, lse_rows, delta_rows, ids_col, ids_row, own, width):
    blocks, ext, _ = proj.shape
    pairs = width // (2 * HEAD)
    rows = lse_rows.shape[1]
    return pl.pallas_call(
        key_kernel,
        grid=(blocks, pairs),
        in_specs=[
            head_block(ext),
            head_block(ext),
            whole_block(rows, ext),
            whole_block(rows, ext),
            head_block(own, pairs),
            head_block(own, 2 * pairs),
            whole_block(own, 1),
            whole_block(1, ext),
        ],
        out_specs=[head_block(own), head_block(own)],
        out_shape=[jax.ShapeDtypeStruct((blocks, own, width), jnp.float32)] * 2,
        name="grad_keys",
    )(proj, grads, lse_rows, delta_rows, proj, proj, ids_col, ids_row)


def flip(x, bit):
    count = lax.axis_size("shard")
    return lax.ppermute(x, "shard", [(i, i ^ bit) for i in range(count)])


def partner(x):
    return flip(x, 1)


def gathered_pieces(piece, chips, after=None):
    rows = piece.shape[0]
    if after is not None:
        piece, after = lax.optimization_barrier((piece, after))
    if chips == 4:
        half = rows // 2
        from_x, from_y = flip(piece, 2), flip(piece, 4)
        upper, lower = flip(from_x[:half], 4), flip(from_y[half:], 2)
        held = [
            (piece, [(0, 0, 0, rows)]),
            (from_x, [(0, 1, 0, rows)]),
            (from_y, [(0, 2, 0, rows)]),
            (upper, [(0, 3, 0, half)]),
            (lower, [(0, 3, half, half)]),
        ]
        return held, (upper, lower)
    held = [(piece, [(0, 0, 0, rows)])]
    step = 1
    while step < chips:
        joined = jnp.concatenate([x for x, _ in held], axis=0)
        spans = [(i * rows, step + i, 0, rows) for i in range(step)]
        held.append((flip(joined, 2 * step), spans))
        step *= 2
    return held, held[-1][0]


def assemble(held, chips, place, plans):
    copies = []
    for index, (_, spans) in enumerate(held):
        for source, which, first, count in spans:
            for target, (rows, parts) in enumerate(plans):
                for who, start, size, column, columns, down, along in parts:
                    low, high = max(first, start), min(first + count, start + size)
                    if low < high:
                        copies.append(
                            (index, source + low - first, high - low, column, columns)
                            + (target, which, who, rows, down + low - start, along)
                        )
    outs = [
        jax.ShapeDtypeStruct(
            (2 * chips * rows, max(p[6] + p[4] for p in parts)), held[0][0].dtype
        )
        for rows, parts in plans
    ]
    n_in = len(held)

    def kernel(place, *refs):
        sources, targets, sems = refs[:n_in], refs[n_in:-1], refs[-1]
        moves = []
        for i, c in enumerate(copies):
            index, row, count, column, columns, target, which, who, rows, down, along = c
            shard = 2 * (place[0] ^ which) + (place[1] ^ who)
            moves.append(
                pltpu.make_async_copy(
                    sources[index].at[pl.ds(row, count), pl.ds(column, columns)],
                    targets[target].at[
                        pl.ds(pl.multiple_of(shard * rows + down, 8), count),
                        pl.ds(along, columns),
                    ],
                    sems.at[i],
                )
            )
        for move in moves:
            move.start()
        for move in moves:
            move.wait()

    return pl.pallas_call(
        kernel,
        in_specs=[pl.BlockSpec(memory_space=pltpu.SMEM)]
        + [pl.BlockSpec(memory_space=pl.ANY)] * n_in,
        out_specs=[pl.BlockSpec(memory_space=pltpu.VMEM)] * len(outs),
        out_shape=outs,
        scratch_shapes=[pltpu.SemaphoreType.DMA((len(copies),))],
    )(place, *[x for x, _ in held])


def gradient_chunks(lefts, right, chips, place, tile, extra=0, into=None, first=0, shift=0, size=None, total=None):
    tokens, wide = lefts[0].shape[0], sum(x.shape[1] for x in lefts)
    size = size or right.shape[1]
    n = wide // chips
    shard = n // 2
    total = into[0].shape[1] if into else (total or size)
    given = list(into) if into else []

    def kernel(place, *refs):
        left_refs, right_ref = refs[: len(lefts)], refs[len(lefts)]
        outs = refs[len(lefts) + 1 + len(given) : -2]
        left_ref, pack_ref = refs[-2:]

        @pl.when(pl.program_id(0) == 0)
        def _():
            for i, ref in enumerate(left_refs):
                x = ref[...]
                if i:
                    x = jnp.concatenate([x[tokens // 2 :], x[: tokens // 2]], axis=0)
                hi, lo = halves(x.T)
                count = chips // len(left_refs)
                for c in range(count):
                    which = c if len(left_refs) == 1 else c + count * (place[1] ^ i)
                    at = pl.ds(pl.multiple_of((place[0] ^ which) * n, 16), n)
                    part = slice(c * n, (c + 1) * n)
                    left_ref[at, :tokens] = lo[part]
                    left_ref[at, tokens : 2 * tokens] = hi[part]
                    left_ref[at, 2 * tokens :] = hi[part]

        hi, lo = halves(right_ref[...])
        pack_ref[:tokens, :] = hi
        pack_ref[tokens : 2 * tokens, :] = lo
        pack_ref[2 * tokens :, :] = hi
        product = jnp.dot(left_ref[...], pack_ref[...], preferred_element_type=jnp.float32)
        for j in range(chips):
            for i in range(2):
                outs[j][i * (shard + extra) : i * (shard + extra) + shard, :] = product[
                    j * n + i * shard : j * n + (i + 1) * shard
                ]

    steps = size // tile
    return pl.pallas_call(
        kernel,
        grid_spec=pltpu.PrefetchScalarGridSpec(
            num_scalar_prefetch=1,
            grid=(steps,),
            in_specs=[pl.BlockSpec(x.shape, lambda i, place: (0, 0)) for x in lefts]
            + [pl.BlockSpec((tokens, tile), lambda i, place: (0, i + place[1] * (shift // tile)))]
            + [pl.BlockSpec(memory_space=pl.ANY) for _ in given],
            out_specs=[
                pl.BlockSpec((n + 2 * extra, tile), lambda i, place: (0, i + first // tile))
            ]
            * chips,
            scratch_shapes=[
                pltpu.VMEM((wide, 3 * tokens), jnp.bfloat16),
                pltpu.VMEM((3 * tokens, tile), jnp.bfloat16),
            ],
        ),
        out_shape=[jax.ShapeDtypeStruct((n + 2 * extra, total), jnp.float32)] * chips,
        input_output_aliases={2 + len(lefts) + i: i for i in range(len(given))},
    )(place, *lefts, right, *given)


def put_rows(chunks, table, place, shard, extra):
    count = len(chunks)

    def kernel(place, table_ref, *refs):
        outs, sems = refs[count:-1], refs[-1]
        moves = [
            pltpu.make_async_copy(
                table_ref.at[
                    pl.ds(pl.multiple_of((2 * (place[0] ^ j) + i) * extra, 8), extra), :
                ],
                outs[j].at[pl.ds(i * (shard + extra) + shard, extra), :],
                sems.at[2 * j + i],
            )
            for j in range(count)
            for i in range(2)
        ]
        for move in moves:
            move.start()
        for move in moves:
            move.wait()

    return pl.pallas_call(
        kernel,
        in_specs=[pl.BlockSpec(memory_space=pltpu.SMEM), pl.BlockSpec(memory_space=pltpu.VMEM)]
        + [pl.BlockSpec(memory_space=pl.ANY)] * count,
        out_specs=[pl.BlockSpec(memory_space=pl.ANY)] * count,
        out_shape=[jax.ShapeDtypeStruct(x.shape, x.dtype) for x in chunks],
        scratch_shapes=[pltpu.SemaphoreType.DMA((2 * count,))],
        input_output_aliases={2 + j: j for j in range(count)},
        name="put_rows",
    )(place, table, *chunks)


def scatter_chunks(chunks):
    n = chunks[0].shape[0]
    if len(chunks) == 4:
        half = n // 2
        via_x = flip(chunks[3][:half], 2)
        via_y = flip(chunks[3][half:], 4)
        to_y = flip(jnp.concatenate([chunks[2][:half] + via_x, chunks[2][half:]]), 4)
        to_x = flip(jnp.concatenate([chunks[1][:half], chunks[1][half:] + via_y]), 2)
        return [chunks[0], to_y, to_x]
    held = list(chunks)
    step = len(held) // 2
    while step:
        other = flip(jnp.concatenate(held[step:], axis=0), 2 * step)
        held = [held[i] + other[i * n : (i + 1) * n] for i in range(step)]
        step //= 2
    return held


def halo_moves(shards, reps):
    own_prev, other_prev, own_next, other_next = [], [], [], []
    for s in range(shards):
        for r in range(reps):
            here = s * reps + r
            if r > 0:
                own_prev.append((here - 1, here))
                other_prev.append((here - 1, here))
            else:
                source = s if s % 2 else s - 2
                if source >= 0:
                    own_prev.append((source * reps + reps - 1, here))
                source = s - 2 if s % 2 else s
                if source >= 0:
                    other_prev.append((source * reps + reps - 1, here))
            if r < reps - 1:
                own_next.append((here + 1, here))
                other_next.append((here + 1, here))
            else:
                source = s + 2 if s % 2 else s
                if source < shards:
                    own_next.append((source * reps, here))
                source = s if s % 2 else s + 2
                if source < shards:
                    other_next.append((source * reps, here))
    return own_prev, other_prev, own_next, other_next


def ordered(mine, theirs, odd, axis):
    size = mine.shape[axis]
    shape = list(mine.shape)
    shape[axis] = 2 * size
    both = jnp.zeros(tuple(shape), mine.dtype)
    both = lax.dynamic_update_slice_in_dim(both, mine, odd * size, axis)
    return lax.dynamic_update_slice_in_dim(both, theirs, (1 - odd) * size, axis)


def swap_halves(x):
    n = x.shape[0] // 2
    return jnp.concatenate([x[n:], x[:n]], axis=0)


def pair_sum(x):
    return x + swap_halves(partner(x))


def pick(x, index, size, axis):
    return lax.dynamic_slice_in_dim(x, index * size, size, axis)


def per_device(
    inputs,
    image_ids,
    output_gradient,
    first_norm_scale,
    first_norm_bias,
    w_qkv,
    bias_query,
    bias_value,
    w_output,
    bias_output,
    second_norm_scale,
    second_norm_bias,
    w_up,
    bias_up,
    w_down,
    bias_down,
):
    shards, reps = lax.axis_size("shard"), lax.axis_size("rep")
    chips = shards // 2
    shard, rep = lax.axis_index("shard"), lax.axis_index("rep")
    chip, odd = shard // 2, shard % 2
    axes = ("shard", "rep")
    own, width = inputs.shape
    rows = w_qkv.shape[0]
    mine = width // 2
    hidden = w_up.shape[1] // 2
    ext = own + 2 * REACH

    ids = (image_ids + 1).astype(jnp.float32)

    def with_ids(x, x_ids):
        line = jnp.pad(x_ids[None], ((0, PAD - 1), (0, width - x_ids.shape[0])))
        return jnp.concatenate([x, line], axis=0)

    forward = [(i, i + 1) for i in range(shards * reps - 1)]
    backward = [(b, a) for a, b in forward]
    low = lax.ppermute(with_ids(inputs[own - REACH :], ids[own - REACH :]), axes, forward)
    high = lax.ppermute(with_ids(inputs[:REACH], ids[:REACH]), axes, backward)
    g_two = jnp.concatenate([output_gradient, partner(output_gradient)], axis=0)

    small = jnp.concatenate(
        [
            first_norm_scale,
            first_norm_bias,
            second_norm_scale,
            second_norm_bias,
            bias_output,
            bias_down,
            bias_query,
            bias_value,
            bias_up,
        ]
    )
    lead = 3 * mine
    place = jnp.stack([chip, odd])
    small = jnp.pad(small, (0, -small.shape[0] % lead)).reshape(-1, lead)
    small = jnp.pad(small, ((0, -small.shape[0] % PAD), (0, 0)))
    extra = small.shape[0]

    def qkv_half(which):
        parts = [pick(w_qkv, 2 * i + which, mine, 1) for i in range(3)]
        return jnp.concatenate([jnp.concatenate(parts, axis=1), small])

    def rest_half(which):
        return [pick(w_up, which, hidden, 1), pick(w_down.T, which, hidden, 1)]

    first = partner(qkv_half(1 - odd))
    first = jnp.concatenate([qkv_half(odd), first])
    theirs = partner(jnp.concatenate(rest_half(1 - odd), axis=1))
    up_half, down_half = rest_half(odd)
    out_pair = jnp.concatenate([w_output[:, :mine], w_output[:, mine:]])
    second = jnp.concatenate(
        [jnp.concatenate([up_half, theirs[:, :hidden]]), out_pair], axis=1
    )
    third = jnp.concatenate([down_half, theirs[:, hidden:]])
    first_held, _ = gathered_pieces(first, chips)

    low, high, _ = lax.optimization_barrier((low, high, first_held[1][0]))
    ids_ext = jnp.concatenate([ids, low[REACH, :REACH], high[REACH, :REACH]])
    x_ext = jnp.concatenate([inputs, low[:REACH], high[:REACH]], axis=0)
    other_ext = partner(with_ids(x_ext, ids_ext))
    ids_two = jnp.stack([ids_ext, other_ext[ext, :ext]])
    ids_col, ids_row = ids_two[:, :own, None], ids_two[:, None, :]
    tokens = jnp.concatenate([x_ext, other_ext[:ext]], axis=0)

    second_held, sent = gathered_pieces(second, chips)
    third_held, sent = gathered_pieces(third, chips, sent)
    per = rows + extra
    wqkv, gathered_small = assemble(
        first_held,
        chips,
        place,
        [
            (rows, [(i, i * per, rows, 0, lead, 0, 0) for i in range(2)]),
            (extra, [(i, i * per + rows, extra, 0, lead, 0, 0) for i in range(2)]),
        ],
    )
    wup, out_own = assemble(
        second_held,
        chips,
        place,
        [
            (rows, [(i, i * rows, rows, 0, hidden, 0, 0) for i in range(2)]),
            (rows, [(0, i * rows, rows, hidden, mine, 0, i * mine) for i in range(2)]),
        ],
    )
    (wdown_t,) = assemble(
        third_held, chips, place, [(rows, [(i, i * rows, rows, 0, hidden, 0, 0) for i in range(2)])]
    )
    by_shard = out_own.reshape(2, chips // 2, 2, rows, width)

    def out_rows_of(half, parity):
        return pick(pick(by_shard, half, 1, 0), parity, 1, 2).reshape(chips // 2, rows, width)

    out_theirs = partner(out_rows_of(1 - odd, odd))
    out_ours = out_rows_of(odd, odd)
    wout = ordered(out_ours, out_theirs, odd, 1).reshape(mine, width)

    table = gathered_small.reshape(shards, extra * lead)

    def vector(start, size):
        return table[:, start : start + size].reshape(shards * size)

    first_scale, first_bias, second_scale, second_bias, bout, bdown, bq, bv = (
        vector(i * rows, rows) for i in range(8)
    )
    bup = pick(vector(8 * rows, bias_up.shape[0]), odd, hidden, 0)
    shift = jnp.concatenate(
        [pick(bq, odd, mine, 0), jnp.zeros((mine,), jnp.float32), pick(bv, odd, mine, 0)]
    )

    first_normalized, first_standardized, first_inverse_deviation = layer_norm_forward(
        tokens, first_scale, first_bias
    )
    proj = (matmul(first_normalized, wqkv) + shift).reshape(2, ext, lead)
    attended, lse = attention_forward(proj, ids_col, ids_row, own, mine)
    out_rows = attended.reshape(2 * own, mine)
    x_two = jnp.concatenate([tokens[:own], tokens[ext : ext + own]], axis=0)
    middle_state = x_two + pair_sum(matmul(out_rows, wout)) + bout

    second_normalized, second_standardized, second_inverse_deviation = layer_norm_forward(
        middle_state, second_scale, second_bias
    )
    pre = matmul(second_normalized, wup) + bup
    act, slope = gelu_parts(pre)
    down = matmul(act, wdown_t, ((1,), (1,)))
    outputs = middle_state[:own] + (down[:own] + partner(down[own:])) + bdown
    down_chunks = gradient_chunks([g_two], act, chips, place, hidden // 3)
    d_pre = matmul(g_two, wdown_t) * slope
    grad_bias_up = jnp.sum(d_pre, axis=0)
    middle_into = gradient_chunks(
        [second_normalized], d_pre, chips, place, mine, total=hidden + mine
    )
    d_second = pair_sum(matmul(d_pre, wup, ((1,), (1,))))
    gradient_middle = g_two + layer_norm_backward(
        d_second, second_standardized, second_inverse_deviation, second_scale
    )

    d_attended = matmul(gradient_middle, wout, ((1,), (1,)))
    other_rows = partner(out_rows)
    middle_chunks = gradient_chunks(
        [out_rows, other_rows],
        gradient_middle,
        chips,
        place,
        mine,
        into=middle_into,
        first=hidden,
        shift=mine,
        size=mine,
    )
    heads = mine // HEAD
    lse_rows = jnp.swapaxes(lse.reshape(2, own, heads, HEAD)[..., 0], 1, 2)
    member = (
        jnp.arange(mine)[None, :] // HEAD == jnp.arange(heads)[:, None]
    ).astype(jnp.float32)
    delta_rows = lax.dot_general(
        member,
        d_attended * out_rows,
        (((1,), (1,)), ((), ())),
        precision=EXACT,
        preferred_element_type=jnp.float32,
    )
    delta_rows = jnp.swapaxes(delta_rows.reshape(heads, 2, own), 0, 1)
    grads = d_attended.reshape(2, own, mine)
    stats = jnp.concatenate([lse_rows, delta_rows], axis=1)
    lines = -2 * heads % PAD + 2 * heads

    def edge(start):
        s = jnp.pad(
            stats[:, :, start : start + REACH],
            ((0, 0), (0, lines - 2 * heads), (0, mine - REACH)),
        )
        return jnp.concatenate([grads[:, start : start + REACH], s], axis=1)

    own_prev, other_prev, own_next, other_next = halo_moves(shards, reps)
    tail, head = edge(own - REACH), edge(0)
    at_end = (rep == reps - 1).astype(jnp.int32)
    at_start = (rep == 0).astype(jnp.int32)

    def block(x, index):
        return lax.dynamic_index_in_dim(x, index, 0, keepdims=False)

    prev = [
        lax.ppermute(block(tail, at_end), axes, own_prev),
        lax.ppermute(block(tail, 1 - at_end), axes, other_prev),
    ]
    following = [
        lax.ppermute(block(head, at_start), axes, own_next),
        lax.ppermute(block(head, 1 - at_start), axes, other_next),
    ]
    d_query = attention_queries(proj, grads, attended, lse, ids_col, ids_row, own, mine)
    grads_ext = jnp.stack(
        [
            jnp.concatenate([grads[b], prev[b][:REACH], following[b][:REACH]], axis=0)
            for b in range(2)
        ]
    )
    stats_ext = jnp.stack(
        [
            jnp.concatenate(
                [
                    stats[b],
                    prev[b][REACH : REACH + 2 * heads, :REACH],
                    following[b][REACH : REACH + 2 * heads, :REACH],
                ],
                axis=1,
            )
            for b in range(2)
        ]
    )
    d_key, d_value = attention_keys(
        proj, grads_ext, stats_ext[:, :heads], stats_ext[:, heads:], ids_col, ids_row, own, mine
    )
    d_proj = jnp.concatenate([d_query, d_key, d_value], axis=2).reshape(2 * own, lead)
    normalized_two = jnp.concatenate(
        [first_normalized[:own], first_normalized[ext : ext + own]], axis=0
    )
    last_chunks = gradient_chunks([normalized_two], d_proj, chips, place, mine, extra=PAD)
    d_first = matmul(d_proj, wqkv, ((1,), (1,)))
    d_first = d_first[:own] + partner(d_first[own:])
    gradient_of_input = gradient_middle[:own] + layer_norm_backward(
        d_first, first_standardized[:own], first_inverse_deviation[:own], first_scale
    )

    sums = jnp.sum(d_proj, axis=0)

    def spread(half):
        full = jnp.zeros((2 * half.shape[0],), jnp.float32)
        return lax.dynamic_update_slice_in_dim(full, half, odd * half.shape[0], 0)

    small_sums = [
        jnp.sum(d_first * first_standardized[:own], axis=0),
        jnp.sum(d_first, axis=0),
        jnp.sum(d_second[:own] * second_standardized[:own], axis=0),
        jnp.sum(d_second[:own], axis=0),
        jnp.sum(gradient_middle[:own], axis=0),
        jnp.sum(output_gradient, axis=0),
        spread(sums[:mine]),
        spread(sums[2 * mine :]),
        spread(grad_bias_up),
    ]
    table = jnp.concatenate([v.reshape(shards, -1) for v in small_sums], axis=1)
    lines = -(-table.shape[1] // lead)
    table = jnp.pad(table, ((0, 0), (0, lines * lead - table.shape[1])))
    table = jnp.pad(table.reshape(shards, lines, lead), ((0, 0), (0, PAD - lines), (0, 0)))
    last_chunks = put_rows(last_chunks, table.reshape(shards * PAD, lead), place, rows, PAD)

    def finish(parts):
        n = parts[0].shape[0] // 2

        def rows_of(which):
            picked = [pick(x, which, n, 0) for x in parts]
            return sum(picked[1:], picked[0])

        theirs = partner(rows_of(1 - odd))
        return rows_of(odd), theirs

    down_mine, down_theirs = finish(scatter_chunks(down_chunks))
    middle_mine, middle_theirs = finish(scatter_chunks(middle_chunks))
    last_mine, last_theirs = finish(scatter_chunks(last_chunks))
    small_mine, small_theirs = last_mine[rows:], last_theirs[rows:]
    last_mine, last_theirs = last_mine[:rows], last_theirs[:rows]

    total_down = lax.psum(ordered(down_mine, down_theirs, odd, 1), "rep")
    total_down_t = total_down.T
    grad_up_total = ordered(middle_mine[:, :hidden], middle_theirs[:, :hidden], odd, 1)
    grad_out_total = ordered(middle_mine[:, hidden:], middle_theirs[:, hidden:], odd, 1)
    grad_up_total, grad_out_total, total_down = lax.optimization_barrier(
        (grad_up_total, grad_out_total, total_down)
    )
    grad_up_total, grad_out_total = lax.psum((grad_up_total, grad_out_total), "rep")
    qkv_total = jnp.concatenate(
        [
            ordered(last_mine[:, i * mine : (i + 1) * mine], last_theirs[:, i * mine : (i + 1) * mine], odd, 1)
            for i in range(3)
        ],
        axis=1,
    )
    qkv_total = jnp.concatenate(
        [qkv_total, (small_mine + small_theirs).reshape(-1, 2 * lead)], axis=0
    )
    qkv_total, grad_up_total, grad_out_total = lax.optimization_barrier(
        (qkv_total, grad_up_total, grad_out_total)
    )
    qkv_total = lax.psum(qkv_total, "rep")
    qkv_total, small_total = qkv_total[:rows], qkv_total[rows:]
    small_total = small_total.reshape(-1)
    small_out = [small_total[i * rows : (i + 1) * rows] for i in range(8)]
    up_bias_out = small_total[8 * rows : 8 * rows + bias_up.shape[0]]
    return (
        outputs,
        gradient_of_input,
        small_out[0],
        small_out[1],
        qkv_total,
        small_out[6],
        small_out[7],
        grad_out_total,
        small_out[4],
        small_out[2],
        small_out[3],
        grad_up_total,
        up_bias_out,
        total_down_t,
        small_out[5],
    )


def solution(mesh):
    placed = (
        P(("shard", "rep"), None),
        P(("shard", "rep")),
        P(("shard", "rep"), None),
        P("shard"),
        P("shard"),
        P("shard", None),
        P("shard"),
        P("shard"),
        P("shard", None),
        P("shard"),
        P("shard"),
        P("shard"),
        P("shard", None),
        P("shard"),
        P(None, "shard"),
        P("shard"),
    )

    return jax.shard_map(
        per_device,
        mesh=mesh,
        in_specs=placed,
        out_specs=(
            P(("shard", "rep"), None),
            P(("shard", "rep"), None),
            P("shard"),
            P("shard"),
            P("shard", None),
            P("shard"),
            P("shard"),
            P("shard", None),
            P("shard"),
            P("shard"),
            P("shard"),
            P("shard", None),
            P("shard"),
            P(None, "shard"),
            P("shard"),
        ),
        check_vma=False,
    )
```

profile of v0, /device:TPU:0, one launch (start us, length us, event | category | flops | bytes accessed | tf_op | source)
XLA Modules:
  0.0 568.2 jit_solution(16208280812934346721)
XLA Ops:
  21.5 5.0 collective-permute-start.3
  33.6 16.2 %collective-permute-done.1 = f32[208,768]{1,0:T(8,128)S(1)} collective-permute-done((f32[208,768]{1,0:T(8,128)S(1)}, f32[208,768]{1,0:T(8,128)S(1)}, u32[]{:S(2)}, u32[]{:S(2)}) %collective-permute-start.1) | collective-permute-done | bytes 639008 | tf_op jit(solution)/shard_map/ppermute | solution.py:489
  58.2 28.1 %collective-permute-done.5.refs_2_ = f32[208,1152]{1,0:T(8,128)S(1)} collective-permute-done((f32[208,1152]{1,0:T(8,128)S(1)}, f32[208,1152]{1,0:T(8,128)S(1)}, u32[]{:S(2)}, u32[]{:S(2)}) %collective-permute-start.5) | collective-permute-done | bytes 958496 | tf_op jit(solution)/shard_map/ppermute | solution.py:203
  116.6 6.3 %shard_map.272 = (f32[768,1536]{1,0:T(8,128)}, f32[768,768]{1,0:T(8,128)}) custom-call(s32[2]{0:T(128)} %pad_add_fusion.place, f32[192,1920]{1,0:T(8,128)} %copy-done.29, f32[192,1920]{1,0:T(8,128)} %copy-done.40, f32[192,1920]{1,0:T(8,128)} %copy-done.41, f32[96,1920]{1,0:T(8,128)} %collective-permute-done.11.refs_3_, f32[96,1920]{1,0:T(8,128)} %copy-done.58), custom_call_target="tpu_custom_call" | custom-call | tf_op jit(solution)/shard_map/pallas_call | solution.py:277
  135.6 10.3 %convolution_add_fusion = f32[1312,1152]{1,0:T(8,128)} fusion(f32[1312,768]{1,0:T(8,128)S(1)} %get-tuple-element.103, f32[768,1152]{1,0:T(8,128)S(1)} %copy-done.38, f32[1152]{0:T(1024)S(1)} %pad_maximum_fusion.17), kind=kOutput, calls=%fused_computation | convolution fusion | flops 6966153216 | bytes 13619712 | tf_op jit(solution)/shard_map/dot_general | solution.py:19
  146.0 11.2 %attend.1 = (f32[2,256,384]{2,1,0:T(8,128)}, f32[2,256,384]{2,1,0:T(8,128)}) custom-call(f32[2,656,1152]{2,1,0:T(8,128)} %bitcast.72, f32[2,656,1152]{2,1,0:T(8,128)} %bitcast.73, f32[2,656,1152]{2,1,0:T(8,128)} %bitcast.74, f32[2,256,1]{2,1,0:T(8,128)} %copy.45.idc_ref, f32[2,1,656]{2,1,0:T(1,128)} %copy.46.idr_ref), custom_call_target="tpu_custom_call" | custom-call | tf_op jit(solution)/shard_map/attend/pallas_call | solution.py:140
  175.2 5.8 %collective-permute-done.17.refs_3_ = f32[96,1536]{1,0:T(8,128)} collective-permute-done((f32[96,1536]{1,0:T(8,128)}, f32[96,1536]{1,0:T(8,128)}, u32[]{:S(2)}, u32[]{:S(2)}) %collective-permute-start.17) | collective-permute-done | bytes 589856 | tf_op jit(solution)/shard_map/ppermute | solution.py:203
  183.4 5.1 shard_map.273
  193.9 5.8 %fusion.25 = (f32[512,1536]{1,0:T(8,128)}, f32[512,1536]{1,0:T(8,128)S(1)}) fusion(f32[1536]{0:T(1024)S(1)} %dynamic_slice.129, f32[512,768]{1,0:T(8,128)S(1)} %get-tuple-element.99.refs_0_, f32[768,1536]{1,0:T(8,128)S(1)} %bitcast.88), kind=kOutput, calls=%fused_computation.156 | convolution fusion | flops 3627810816 | bytes 12589056 | tf_op jit(solution)/shard_map/dot_general | solution.py:19
  199.7 8.4 %shard_map.277 = (f32[192,1536]{1,0:T(8,128)}, f32[192,1536]{1,0:T(8,128)}, f32[192,1536]{1,0:T(8,128)}, f32[192,1536]{1,0:T(8,128)}) custom-call(s32[2]{0:T(128)} %pad_add_fusion.place, f32[512,768]{1,0:T(8,128)} %copy-done.12, f32[512,1536]{1,0:T(8,128)} %get-tuple-element.192.refs_1_), custom_call_target="tpu_custom_call" | custom-call | tf_op jit(solution)/shard_map/pallas_call | solution.py:328
  212.0 8.0 %fusion.46 = (f32[1536]{0:T(1024)S(1)}, f32[512,1536]{1,0:T(8,128)}) fusion(f32[512,1536]{1,0:T(8,128)S(1)} %get-tuple-element.193, f32[512,768]{1,0:T(8,128)S(1)} %copy-done.13, f32[768,1536]{1,0:T(8,128)} %shard_map.273), kind=kOutput, calls=%fused_computation.176 | convolution fusion | flops 3631741440 | bytes 12589056 | tf_op jit(solution)/shard_map/dot_general | solution.py:19
  225.6 9.9 %shard_map.275 = (f32[192,1920]{1,0:T(8,128)}, f32[192,1920]{1,0:T(8,128)}, f32[192,1920]{1,0:T(8,128)}, f32[192,1920]{1,0:T(8,128)}) custom-call(s32[2]{0:T(128)} %pad_add_fusion.place, f32[512,768]{1,0:T(8,128)} %copy-done.17, f32[512,1536]{1,0:T(8,128)} %get-tuple-element.195.refs_1_), custom_call_target="tpu_custom_call" | custom-call | tf_op jit(solution)/shard_map/pallas_call | solution.py:328
  235.5 7.5 %fusion.49 = f32[512,768]{1,0:T(8,128)} fusion(f32[512,1536]{1,0:T(8,128)S(1)} %copy-done.2, f32[768,1536]{1,0:T(8,128)} %get-tuple-element.57), kind=kOutput, calls=%fused_computation.179 | convolution fusion | flops 3623878656 | bytes 9437184 | tf_op jit(solution)/shard_map/dot_general | solution.py:19
  248.4 11.7 %collective-permute-done.38 = f32[96,1536]{1,0:T(8,128)S(1)} collective-permute-done((f32[96,1536]{1,0:T(8,128)}, f32[96,1536]{1,0:T(8,128)S(1)}, u32[]{:S(2)}, u32[]{:S(2)}) %collective-permute-start.38) | collective-permute-done | bytes 589856 | tf_op jit(solution)/shard_map/ppermute | solution.py:203
  268.7 10.6 %grad_queries.1 = f32[2,256,384]{2,1,0:T(8,128)} custom-call(f32[2,656,1152]{2,1,0:T(8,128)} %bitcast.75, f32[2,656,1152]{2,1,0:T(8,128)} %bitcast.76, f32[2,656,1152]{2,1,0:T(8,128)} %bitcast.77, f32[2,256,384]{2,1,0:T(8,128)} %bitcast.84, f32[2,256,384]{2,1,0:T(8,128)} %get-tuple-element.55.out_ref, f32[2,256,384]{2,1,0:T(8,128)} %get-tuple-element.59.lse_ref, ...), custom_call_target="tpu_custom_call" | custom-call | tf_op jit(solution)/shard_map/grad_queries/pallas_call | solution.py:159
  294.1 5.2 shard_map.276
  307.0 4.8 collective-permute-start.35
  319.4 13.1 %grad_keys.1 = (f32[2,256,384]{2,1,0:T(8,128)}, f32[2,256,384]{2,1,0:T(8,128)}) custom-call(f32[2,656,1152]{2,1,0:T(8,128)} %bitcast.78, f32[2,656,384]{2,1,0:T(8,128)} %pad_maximum_fusion.2.g_ref, f32[2,6,656]{2,1,0:T(8,128)} %get-tuple-element.177.lse_ref, f32[2,6,656]{2,1,0:T(8,128)} %get-tuple-element.176.delta_ref, f32[2,656,1152]{2,1,0:T(8,128)} %bitcast.79, ...), custom_call_target="tpu_custom_call" | custom-call | tf_op jit(solution)/shard_map/grad_keys/pallas_call | solution.py:182
  357.4 8.2 %shard_map.274 = (f32[208,1152]{1,0:T(8,128)}, f32[208,1152]{1,0:T(8,128)}, f32[208,1152]{1,0:T(8,128)}, f32[208,1152]{1,0:T(8,128)}) custom-call(s32[2]{0:T(128)} %pad_add_fusion.place, f32[512,768]{1,0:T(8,128)} %pad_maximum_fusion.3.refs_0_, f32[512,1152]{1,0:T(8,128)} %bitcast.86), custom_call_target="tpu_custom_call" | custom-call | tf_op jit(solution)/shard_map/pallas_call | solution.py:328
  377.8 7.1 %collective-permute-done.29 = f32[104,1152]{1,0:T(8,128)S(1)} collective-permute-done((f32[104,1152]{1,0:T(8,128)}, f32[104,1152]{1,0:T(8,128)S(1)}, u32[]{:S(2)}, u32[]{:S(2)}) %collective-permute-start.29) | collective-permute-done | bytes 479264 | tf_op jit(solution)/shard_map/ppermute | solution.py:203
  395.0 21.6 %collective-permute-done.34 = f32[192,1920]{1,0:T(8,128)} collective-permute-done((f32[192,1920]{1,0:T(8,128)}, f32[192,1920]{1,0:T(8,128)}, u32[]{:S(2)}, u32[]{:S(2)}) %collective-permute-start.34) | collective-permute-done | bytes 1474592 | tf_op jit(solution)/shard_map/ppermute | solution.py:203
  419.0 17.5 %collective-permute-done.28 = f32[208,1152]{1,0:T(8,128)S(1)} collective-permute-done((f32[208,1152]{1,0:T(8,128)S(1)}, f32[208,1152]{1,0:T(8,128)S(1)}, u32[]{:S(2)}, u32[]{:S(2)}) %collective-permute-start.28) | collective-permute-done | bytes 958496 | tf_op jit(solution)/shard_map/ppermute | solution.py:203
  445.1 57.6 %all-reduce.16.cloned.1.call-done = (f32[96,3072]{1,0:T(8,128)}, f32[96,768]{1,0:T(8,128)}) async-done(((f32[96,3072]{1,0:T(8,128)}, f32[96,768]{1,0:T(8,128)}), (f32[96,3072]{1,0:T(8,128)}, f32[96,768]{1,0:T(8,128)})) %all-reduce.16.cloned.1.call-update) | async-done | bytes 1474576 | tf_op jit(solution)/shard_map/psum | solution.py:743
  505.0 49.6 %all-reduce.14.cloned.1.call-done = f32[100,2304]{1,0:T(8,128)} async-done(((f32[100,2304]{1,0:T(8,128)}), f32[100,2304]{1,0:T(8,128)}) %all-reduce.14.cloned.1.call-update) | async-done | bytes 921616 | tf_op jit(solution)/shard_map/psum | solution.py:757
  (412 shorter events, 218.3 us)
Async XLA Ops:
  7.2 430.4 %all-reduce.12.cloned.1.call-start = ((), (), s32[]{:S(2)}) async-start(), calls=%async_computation | async-start | bytes 2359296 | tf_op jit(solution)/shard_map/psum | solution.py:736
  21.5 31.9 %collective-permute-start.3 = (f32[208,1152]{1,0:T(8,128)S(1)}, f32[208,1152]{1,0:T(8,128)S(1)}, u32[]{:S(2)}, u32[]{:S(2)}) collective-permute-start(f32[208,1152]{1,0:T(8,128)S(1)} %pad_maximum_fusion.10.refs_0_), channel_id=1, source_target_pairs={{0,8},{4,12},{8,0},{12,4},{16,24},{20,28},{24,16},{28,20},{1,9},{5... | collective-permute-start | bytes 2875400 | tf_op jit(solution)/shard_map/ppermute | solution.py:203
  27.5 59.6 %collective-permute-start.9 = (f32[192,1920]{1,0:T(8,128)S(1)}, f32[192,1920]{1,0:T(8,128)S(1)}, u32[]{:S(2)}, u32[]{:S(2)}) collective-permute-start(f32[192,1920]{1,0:T(8,128)S(1)} %maximum_maximum_fusion.refs_0_), channel_id=1, source_target_pairs={{0,8},{4,12},{8,0},{12,4},{16,24},{20,28},{24,16},{28,20},{1,9},{5... | collective-permute-start | bytes 4423688 | tf_op jit(solution)/shard_map/ppermute | solution.py:203
  27.7 62.9 %collective-permute-start.10 = (f32[192,1920]{1,0:T(8,128)S(1)}, f32[192,1920]{1,0:T(8,128)S(1)}, u32[]{:S(2)}, u32[]{:S(2)}) collective-permute-start(f32[192,1920]{1,0:T(8,128)S(1)} %maximum_maximum_fusion.refs_0_), channel_id=1, source_target_pairs={{0,16},{4,20},{8,24},{12,28},{16,0},{20,4},{24,8},{28,12},{1,17},{... | collective-permute-start | bytes 4423688 | tf_op jit(solution)/shard_map/ppermute | solution.py:203
  55.2 70.9 %collective-permute-start.4 = (f32[664,768]{1,0:T(8,128)}, f32[664,768]{1,0:T(8,128)}, u32[]{:S(2)}, u32[]{:S(2)}) collective-permute-start(f32[664,768]{1,0:T(8,128)} %select_maximum_fusion), channel_id=1, source_target_pairs={{0,4},{4,0},{8,12},{12,8},{16,20},{20,16},{24,28},{28,24},{1,5},{5... | collective-permute-start | bytes 6119432 | tf_op jit(solution)/shard_map/ppermute | solution.py:203
  55.2 31.0 %collective-permute-start.5 = (f32[208,1152]{1,0:T(8,128)S(1)}, f32[208,1152]{1,0:T(8,128)S(1)}, u32[]{:S(2)}, u32[]{:S(2)}) collective-permute-start(f32[208,1152]{1,0:T(8,128)S(1)} %pad_maximum_fusion.10.refs_0_), channel_id=1, source_target_pairs={{0,16},{4,20},{8,24},{12,28},{16,0},{20,4},{24,8},{28,12},{1,17},{... | collective-permute-start | bytes 2875400 | tf_op jit(solution)/shard_map/ppermute | solution.py:203
  56.5 40.2 %collective-permute-start.6 = (f32[104,1152]{1,0:T(8,128)}, f32[104,1152]{1,0:T(8,128)}, u32[]{:S(2)}, u32[]{:S(2)}) collective-permute-start(f32[104,1152]{1,0:T(8,128)} %slice.453), channel_id=1, source_target_pairs={{0,16},{4,20},{8,24},{12,28},{16,0},{20,4},{24,8},{28,12},{1,17},{... | collective-permute-start | bytes 1437704 | tf_op jit(solution)/shard_map/ppermute | solution.py:203
  114.1 49.0 %collective-permute-start.15 = (f32[192,1536]{1,0:T(8,128)}, f32[192,1536]{1,0:T(8,128)}, u32[]{:S(2)}, u32[]{:S(2)}) collective-permute-start(f32[192,1536]{1,0:T(8,128)} %pad_maximum_fusion.7.refs_0_), channel_id=1, source_target_pairs={{0,8},{4,12},{8,0},{12,4},{16,24},{20,28},{24,16},{28,20},{1,9},{5... | collective-permute-start | bytes 3538952 | tf_op jit(solution)/shard_map/ppermute | solution.py:203
  114.1 51.7 %collective-permute-start.16 = (f32[192,1536]{1,0:T(8,128)}, f32[192,1536]{1,0:T(8,128)}, u32[]{:S(2)}, u32[]{:S(2)}) collective-permute-start(f32[192,1536]{1,0:T(8,128)} %pad_maximum_fusion.7.refs_0_), channel_id=1, source_target_pairs={{0,16},{4,20},{8,24},{12,28},{16,0},{20,4},{24,8},{28,12},{1,17},{... | collective-permute-start | bytes 3538952 | tf_op jit(solution)/shard_map/ppermute | solution.py:203
  124.8 32.4 %collective-permute-start.13 = (f32[2,96,768]{2,1,0:T(8,128)}, f32[2,96,768]{2,1,0:T(8,128)}, u32[]{:S(2)}, u32[]{:S(2)}) collective-permute-start(f32[2,96,768]{2,1,0:T(8,128)} %dynamic-slice_bitcast_fusion.1), channel_id=1, source_target_pairs={{0,4},{4,0},{8,12},{12,8},{16,20},{20,16},{24,28},{28,24},{1,5},{5... | collective-permute-start | bytes 1769480 | tf_op jit(solution)/shard_map/ppermute | solution.py:203
  171.7 117.6 %collective-permute-start.32 = (f32[512,384]{1,0:T(8,128)}, f32[512,384]{1,0:T(8,128)}, u32[]{:S(2)}, u32[]{:S(2)}) collective-permute-start(f32[512,384]{1,0:T(8,128)} %bitcast.9.refs_0_), channel_id=1, source_target_pairs={{0,4},{4,0},{8,12},{12,8},{16,20},{20,16},{24,28},{28,24},{1,5},{5... | collective-permute-start | bytes 2359304 | tf_op jit(solution)/shard_map/ppermute | solution.py:203
  210.6 34.9 %collective-permute-start.40 = (f32[96,1536]{1,0:T(8,128)}, f32[96,1536]{1,0:T(8,128)}, u32[]{:S(2)}, u32[]{:S(2)}) collective-permute-start(f32[96,1536]{1,0:T(8,128)} %get-tuple-element.130), channel_id=1, source_target_pairs={{0,16},{4,20},{8,24},{12,28},{16,0},{20,4},{24,8},{28,12},{1,17},{... | collective-permute-start | bytes 1769480 | tf_op jit(solution)/shard_map/ppermute | solution.py:203
  248.1 53.8 %collective-permute-start.41 = (f32[192,1536]{1,0:T(8,128)}, f32[192,1536]{1,0:T(8,128)}, u32[]{:S(2)}, u32[]{:S(2)}) collective-permute-start(f32[192,1536]{1,0:T(8,128)} %pad_maximum_fusion.9), channel_id=1, source_target_pairs={{0,8},{4,12},{8,0},{12,4},{16,24},{20,28},{24,16},{28,20},{1,9},{5... | collective-permute-start | bytes 3538952 | tf_op jit(solution)/shard_map/ppermute | solution.py:203
  261.4 40.6 %collective-permute-start.39 = (f32[192,1536]{1,0:T(8,128)}, f32[192,1536]{1,0:T(8,128)}, u32[]{:S(2)}, u32[]{:S(2)}) collective-permute-start(f32[192,1536]{1,0:T(8,128)} %pad_maximum_fusion.8), channel_id=1, source_target_pairs={{0,16},{4,20},{8,24},{12,28},{16,0},{20,4},{24,8},{28,12},{1,17},{... | collective-permute-start | bytes 3538952 | tf_op jit(solution)/shard_map/ppermute | solution.py:203
  302.0 200.8 %collective-permute-start.19 = (f32[256,768]{1,0:T(8,128)}, f32[256,768]{1,0:T(8,128)}, u32[]{:S(2)}, u32[]{:S(2)}) collective-permute-start(f32[256,768]{1,0:T(8,128)} %slice.476), channel_id=1, source_target_pairs={{0,4},{4,0},{8,12},{12,8},{16,20},{20,16},{24,28},{28,24},{1,5},{5... | collective-permute-start | bytes 2359304 | tf_op jit(solution)/shard_map/ppermute | solution.py:203
  307.0 33.2 %collective-permute-start.35 = (f32[96,1920]{1,0:T(8,128)}, f32[96,1920]{1,0:T(8,128)}, u32[]{:S(2)}, u32[]{:S(2)}) collective-permute-start(f32[96,1920]{1,0:T(8,128)} %get-tuple-element.124), channel_id=1, source_target_pairs={{0,16},{4,20},{8,24},{12,28},{16,0},{20,4},{24,8},{28,12},{1,17},{... | collective-permute-start | bytes 2211848 | tf_op jit(solution)/shard_map/ppermute | solution.py:203
  312.8 33.7 %collective-permute-start.33 = (f32[96,1920]{1,0:T(8,128)}, f32[96,1920]{1,0:T(8,128)}, u32[]{:S(2)}, u32[]{:S(2)}) collective-permute-start(f32[96,1920]{1,0:T(8,128)} %get-tuple-element.123), channel_id=1, source_target_pairs={{0,8},{4,12},{8,0},{12,4},{16,24},{20,28},{24,16},{28,20},{1,9},{5... | collective-permute-start | bytes 2211848 | tf_op jit(solution)/shard_map/ppermute | solution.py:203
  315.4 58.7 %collective-permute-start.42 = (f32[96,1536]{1,0:T(8,128)}, f32[96,1536]{1,0:T(8,128)}, u32[]{:S(2)}, u32[]{:S(2)}) collective-permute-start(f32[96,1536]{1,0:T(8,128)} %get-tuple-element.109), channel_id=1, source_target_pairs={{0,4},{4,0},{8,12},{12,8},{16,20},{20,16},{24,28},{28,24},{1,5},{5... | collective-permute-start | bytes 1769480 | tf_op jit(solution)/shard_map/ppermute | solution.py:203
  342.7 52.3 %collective-permute-start.36 = (f32[192,1920]{1,0:T(8,128)}, f32[192,1920]{1,0:T(8,128)}, u32[]{:S(2)}, u32[]{:S(2)}) collective-permute-start(f32[192,1920]{1,0:T(8,128)} %pad_maximum_fusion.5), channel_id=1, source_target_pairs={{0,8},{4,12},{8,0},{12,4},{16,24},{20,28},{24,16},{28,20},{1,9},{5... | collective-permute-start | bytes 4423688 | tf_op jit(solution)/shard_map/ppermute | solution.py:203
  374.1 42.5 %collective-permute-start.34 = (f32[192,1920]{1,0:T(8,128)}, f32[192,1920]{1,0:T(8,128)}, u32[]{:S(2)}, u32[]{:S(2)}) collective-permute-start(f32[192,1920]{1,0:T(8,128)} %pad_maximum_fusion.4), channel_id=1, source_target_pairs={{0,16},{4,20},{8,24},{12,28},{16,0},{20,4},{24,8},{28,12},{1,17},{... | collective-permute-start | bytes 4423688 | tf_op jit(solution)/shard_map/ppermute | solution.py:203
  376.3 126.4 %all-reduce.16.cloned.1.call-start = ((), (), s32[]{:S(2)}) async-start(), calls=%async_computation.2 | async-start | bytes 2949120 | tf_op jit(solution)/shard_map/psum | solution.py:743
  385.0 33.9 %collective-permute-start.30 = (f32[208,1152]{1,0:T(8,128)S(1)}, f32[208,1152]{1,0:T(8,128)S(1)}, u32[]{:S(2)}, u32[]{:S(2)}) collective-permute-start(f32[208,1152]{1,0:T(8,128)S(1)} %pad_maximum_fusion.12), channel_id=1, source_target_pairs={{0,8},{4,12},{8,0},{12,4},{16,24},{20,28},{24,16},{28,20},{1,9},{5... | collective-permute-start | bytes 2875400 | tf_op jit(solution)/shard_map/ppermute | solution.py:203
  390.4 46.0 %collective-permute-start.28 = (f32[208,1152]{1,0:T(8,128)S(1)}, f32[208,1152]{1,0:T(8,128)S(1)}, u32[]{:S(2)}, u32[]{:S(2)}) collective-permute-start(f32[208,1152]{1,0:T(8,128)S(1)} %pad_maximum_fusion.11), channel_id=1, source_target_pairs={{0,16},{4,20},{8,24},{12,28},{16,0},{20,4},{24,8},{28,12},{1,17},{... | collective-permute-start | bytes 2875400 | tf_op jit(solution)/shard_map/ppermute | solution.py:203
  438.7 115.9 %all-reduce.14.cloned.1.call-start = ((), (), s32[]{:S(2)}) async-start(), calls=%async_computation.1 | async-start | bytes 1916928 | tf_op jit(solution)/shard_map/psum | solution.py:757
  (94 other events, 1056.1 us)
Sparse Core Ops, SparseCore 0:
  376.4 54.4 all-reduce.11
  438.8 63.8 all-reduce.15
  505.7 48.8 all-reduce.13
where the time goes:
time: 579 us; the launch traced here: 568 us
  waiting for transfers between devices  239 us (41%)
  Pallas kernels  84.6 us (15%)
  local copies, waits for them, and re-layouts  66.5 us (11%)
  starting transfers between devices  65 us (11%)
  other arithmetic  50.9 us (9%)
  matrix products  46.6 us (8%)
  between operations  15.2 us (3%)
    ppermute x37, waiting for transfers between devices, flip(): return lax.ppermute(x, 'shard', [(i, i ^ bit) for i in range(count)])  113 us
    psum x1, waiting for transfers between devices, per_device(): lax.psum((grad_up_total, grad_out_total), 'rep')  57.6 us
    psum x1, waiting for transfers between devices, per_device(): qkv_total = lax.psum(qkv_total, 'rep')  49.6 us
    ppermute x37, starting transfers between devices, flip(): return lax.ppermute(x, 'shard', [(i, i ^ bit) for i in range(count)])  46.2 us
    dot_general x8, matrix products, matmul(): lax.dot_general(left, right, (dims, ((), ())), precision=HIGH, preferred_...  44.7 us
    pallas_call x4, Pallas kernels, gradient_chunks(): pl.pallas_call(kernel, grid_spec=pltpu.PrefetchScalarGridSpec(num_scalar_...  31.7 us
    pallas_call x3, Pallas kernels, assemble(): pl.pallas_call(kernel, in_specs=[pl.BlockSpec(memory_space=pltpu.SMEM)] +...  16.2 us
    ppermute x1, waiting for transfers between devices, per_device(): high = lax.ppermute(with_ids(inputs[:REACH], ids[:REACH]), axes, backward)  16.2 us
  transfers between devices with their start and end apart: 46, of which 17 were waited for; matrix products, arithmetic and copies ran while one was open for 25% of the time, Pallas kernels for 15%

commit v1 on v0

--- a/solution.py
+++ b/solution.py
@@ -13,6 +13,9 @@
 PAD = 8
 HIGH = lax.Precision.HIGH
 EXACT = lax.Precision.HIGHEST
+
+
+SHARD, REP = "shard", "rep"
 
 
 def matmul(left, right, dims=((1,), (0,))):
@@ -149,7 +152,7 @@
         ],
         out_specs=[head_block(own), head_block(own)],
         out_shape=[jax.ShapeDtypeStruct((blocks, own, width), jnp.float32)] * 2,
-        name="attend",
+        name="af",
     )(proj, proj, proj, ids_col, ids_row)
 
 
@@ -171,7 +174,7 @@
         ],
         out_specs=head_block(own),
         out_shape=jax.ShapeDtypeStruct((blocks, own, width), jnp.float32),
-        name="grad_queries",
+        name="aq",
     )(proj, proj, proj, grads, out, lse, ids_col, ids_row)
 
 
@@ -194,13 +197,13 @@
         ],
         out_specs=[head_block(own), head_block(own)],
         out_shape=[jax.ShapeDtypeStruct((blocks, own, width), jnp.float32)] * 2,
-        name="grad_keys",
+        name="ak",
     )(proj, grads, lse_rows, delta_rows, proj, proj, ids_col, ids_row)
 
 
 def flip(x, bit):
-    count = lax.axis_size("shard")
-    return lax.ppermute(x, "shard", [(i, i ^ bit) for i in range(count)])
+    count = lax.axis_size(SHARD)
+    return lax.ppermute(x, SHARD, [(i, i ^ bit) for i in range(count)])
 
 
 def partner(x):
@@ -376,7 +379,7 @@
         out_shape=[jax.ShapeDtypeStruct(x.shape, x.dtype) for x in chunks],
         scratch_shapes=[pltpu.SemaphoreType.DMA((2 * count,))],
         input_output_aliases={2 + j: j for j in range(count)},
-        name="put_rows",
+        name="pr",
     )(place, table, *chunks)
 
 
@@ -466,11 +469,11 @@
     w_down,
     bias_down,
 ):
-    shards, reps = lax.axis_size("shard"), lax.axis_size("rep")
+    shards, reps = lax.axis_size(SHARD), lax.axis_size(REP)
     chips = shards // 2
-    shard, rep = lax.axis_index("shard"), lax.axis_index("rep")
+    shard, rep = lax.axis_index(SHARD), lax.axis_index(REP)
     chip, odd = shard // 2, shard % 2
-    axes = ("shard", "rep")
+    axes = (SHARD, REP)
     own, width = inputs.shape
     rows = w_qkv.shape[0]
     mine = width // 2
@@ -583,7 +586,8 @@
     first_normalized, first_standardized, first_inverse_deviation = layer_norm_forward(
         tokens, first_scale, first_bias
     )
-    proj = (matmul(first_normalized, wqkv) + shift).reshape(2, ext, lead)
+    proj = matmul(first_normalized, wqkv) + shift
+    proj = proj.reshape(2, ext, lead)
     attended, lse = attention_forward(proj, ids_col, ids_row, own, mine)
     out_rows = attended.reshape(2 * own, mine)
     x_two = jnp.concatenate([tokens[:own], tokens[ext : ext + own]], axis=0)
@@ -733,14 +737,14 @@
     small_mine, small_theirs = last_mine[rows:], last_theirs[rows:]
     last_mine, last_theirs = last_mine[:rows], last_theirs[:rows]
 
-    total_down = lax.psum(ordered(down_mine, down_theirs, odd, 1), "rep")
+    total_down = lax.psum(ordered(down_mine, down_theirs, odd, 1), REP)
     total_down_t = total_down.T
     grad_up_total = ordered(middle_mine[:, :hidden], middle_theirs[:, :hidden], odd, 1)
     grad_out_total = ordered(middle_mine[:, hidden:], middle_theirs[:, hidden:], odd, 1)
     grad_up_total, grad_out_total, total_down = lax.optimization_barrier(
         (grad_up_total, grad_out_total, total_down)
     )
-    grad_up_total, grad_out_total = lax.psum((grad_up_total, grad_out_total), "rep")
+    grad_up_total, grad_out_total = lax.psum((grad_up_total, grad_out_total), REP)
     qkv_total = jnp.concatenate(
         [
             ordered(last_mine[:, i * mine : (i + 1) * mine], last_theirs[:, i * mine : (i + 1) * mine], odd, 1)
@@ -754,7 +758,7 @@
     qkv_total, grad_up_total, grad_out_total = lax.optimization_barrier(
         (qkv_total, grad_up_total, grad_out_total)
     )
-    qkv_total = lax.psum(qkv_total, "rep")
+    qkv_total = lax.psum(qkv_total, REP)
     qkv_total, small_total = qkv_total[:rows], qkv_total[rows:]
     small_total = small_total.reshape(-1)
     small_out = [small_total[i * rows : (i + 1) * rows] for i in range(8)]
@@ -780,22 +784,22 @@
 
 def solution(mesh):
     placed = (
-        P(("shard", "rep"), None),
-        P(("shard", "rep")),
-        P(("shard", "rep"), None),
-        P("shard"),
-        P("shard"),
-        P("shard", None),
-        P("shard"),
-        P("shard"),
-        P("shard", None),
-        P("shard"),
-        P("shard"),
-        P("shard"),
-        P("shard", None),
-        P("shard"),
-        P(None, "shard"),
-        P("shard"),
+        P((SHARD, REP), None),
+        P((SHARD, REP)),
+        P((SHARD, REP), None),
+        P(SHARD),
+        P(SHARD),
+        P(SHARD, None),
+        P(SHARD),
+        P(SHARD),
+        P(SHARD, None),
+        P(SHARD),
+        P(SHARD),
+        P(SHARD),
+        P(SHARD, None),
+        P(SHARD),
+        P(None, SHARD),
+        P(SHARD),
     )
 
     return jax.shard_map(
@@ -803,21 +807,21 @@
         mesh=mesh,
         in_specs=placed,
         out_specs=(
-            P(("shard", "rep"), None),
-            P(("shard", "rep"), None),
-            P("shard"),
-            P("shard"),
-            P("shard", None),
-            P("shard"),
-            P("shard"),
-            P("shard", None),
-            P("shard"),
-            P("shard"),
-            P("shard"),
-            P("shard", None),
-            P("shard"),
-            P(None, "shard"),
-            P("shard"),
+            P((SHARD, REP), None),
+            P((SHARD, REP), None),
+            P(SHARD),
+            P(SHARD),
+            P(SHARD, None),
+            P(SHARD),
+            P(SHARD),
+            P(SHARD, None),
+            P(SHARD),
+            P(SHARD),
+            P(SHARD),
+            P(SHARD, None),
+            P(SHARD),
+            P(None, SHARD),
+            P(SHARD),
         ),
         check_vma=False,
     )

time: 579 us -> 579 us (level)
  no operation moved by 1% of the time
where the time goes in v1:
time: 579 us; the launch traced here: 568 us
  waiting for transfers between devices  239 us (41%)
  Pallas kernels  84.6 us (15%)
  local copies, waits for them, and re-layouts  66.5 us (11%)
  starting transfers between devices  65 us (11%)
  other arithmetic  50.9 us (9%)
  matrix products  46.6 us (8%)
  between operations  15.2 us (3%)
    ppermute x37, waiting for transfers between devices, flip(): return lax.ppermute(x, SHARD, [(i, i ^ bit) for i in range(count)])  113 us
    psum x1, waiting for transfers between devices, per_device(): lax.psum((grad_up_total, grad_out_total), REP)  57.6 us
    psum x1, waiting for transfers between devices, per_device(): qkv_total = lax.psum(qkv_total, REP)  49.6 us
    ppermute x37, starting transfers between devices, flip(): return lax.ppermute(x, SHARD, [(i, i ^ bit) for i in range(count)])  46.2 us
    dot_general x8, matrix products, matmul(): lax.dot_general(left, right, (dims, ((), ())), precision=HIGH, preferred_...  44.7 us
    pallas_call x4, Pallas kernels, gradient_chunks(): pl.pallas_call(kernel, grid_spec=pltpu.PrefetchScalarGridSpec(num_scalar_...  31.7 us
    pallas_call x3, Pallas kernels, assemble(): pl.pallas_call(kernel, in_specs=[pl.BlockSpec(memory_space=pltpu.SMEM)] +...  16.2 us
    ppermute x1, waiting for transfers between devices, per_device(): high = lax.ppermute(with_ids(inputs[:REACH], ids[:REACH]), axes, backward)  16.2 us
  transfers between devices with their start and end apart: 46, of which 17 were waited for; matrix products, arithmetic and copies ran while one was open for 25% of the time, Pallas kernels for 15%

profile of v1, /device:TPU:0, one launch (start us, length us, event | category | flops | bytes accessed | tf_op | source)
XLA Modules:
  0.0 568.2 jit_solution(16208280812934346721)
XLA Ops:
  21.5 5.0 collective-permute-start.3
  33.6 16.2 %collective-permute-done.1 = f32[208,768]{1,0:T(8,128)S(1)} collective-permute-done((f32[208,768]{1,0:T(8,128)S(1)}, f32[208,768]{1,0:T(8,128)S(1)}, u32[]{:S(2)}, u32[]{:S(2)}) %collective-permute-start.1) | collective-permute-done | bytes 639008 | tf_op jit(solution)/shard_map/ppermute | solution.py:492
  58.2 28.1 %collective-permute-done.5.refs_2_ = f32[208,1152]{1,0:T(8,128)S(1)} collective-permute-done((f32[208,1152]{1,0:T(8,128)S(1)}, f32[208,1152]{1,0:T(8,128)S(1)}, u32[]{:S(2)}, u32[]{:S(2)}) %collective-permute-start.5) | collective-permute-done | bytes 958496 | tf_op jit(solution)/shard_map/ppermute | solution.py:206
  116.6 6.3 %shard_map.272 = (f32[768,1536]{1,0:T(8,128)}, f32[768,768]{1,0:T(8,128)}) custom-call(s32[2]{0:T(128)} %pad_add_fusion.place, f32[192,1920]{1,0:T(8,128)} %copy-done.29, f32[192,1920]{1,0:T(8,128)} %copy-done.40, f32[192,1920]{1,0:T(8,128)} %copy-done.41, f32[96,1920]{1,0:T(8,128)} %collective-permute-done.11.refs_3_, f32[96,1920]{1,0:T(8,128)} %copy-done.58), custom_call_target="tpu_custom_call" | custom-call | tf_op jit(solution)/shard_map/pallas_call | solution.py:280
  135.6 10.3 %convolution_add_fusion = f32[1312,1152]{1,0:T(8,128)} fusion(f32[1312,768]{1,0:T(8,128)S(1)} %get-tuple-element.103, f32[768,1152]{1,0:T(8,128)S(1)} %copy-done.38, f32[1152]{0:T(1024)S(1)} %pad_maximum_fusion.17), kind=kOutput, calls=%fused_computation | convolution fusion | flops 6966153216 | bytes 13619712 | tf_op jit(solution)/shard_map/dot_general | solution.py:22
  146.0 11.2 %af.1 = (f32[2,256,384]{2,1,0:T(8,128)}, f32[2,256,384]{2,1,0:T(8,128)}) custom-call(f32[2,656,1152]{2,1,0:T(8,128)} %bitcast.72, f32[2,656,1152]{2,1,0:T(8,128)} %bitcast.73, f32[2,656,1152]{2,1,0:T(8,128)} %bitcast.74, f32[2,256,1]{2,1,0:T(8,128)} %copy.45.idc_ref, f32[2,1,656]{2,1,0:T(1,128)} %copy.46.idr_ref), custom_call_target="tpu_custom_call" | custom-call | tf_op jit(solution)/shard_map/af/pallas_call | solution.py:143
  175.2 5.8 %collective-permute-done.17.refs_3_ = f32[96,1536]{1,0:T(8,128)} collective-permute-done((f32[96,1536]{1,0:T(8,128)}, f32[96,1536]{1,0:T(8,128)}, u32[]{:S(2)}, u32[]{:S(2)}) %collective-permute-start.17) | collective-permute-done | bytes 589856 | tf_op jit(solution)/shard_map/ppermute | solution.py:206
  183.4 5.1 shard_map.273
  193.9 5.8 %fusion.25 = (f32[512,1536]{1,0:T(8,128)}, f32[512,1536]{1,0:T(8,128)S(1)}) fusion(f32[1536]{0:T(1024)S(1)} %dynamic_slice.129, f32[512,768]{1,0:T(8,128)S(1)} %get-tuple-element.99.refs_0_, f32[768,1536]{1,0:T(8,128)S(1)} %bitcast.88), kind=kOutput, calls=%fused_computation.156 | convolution fusion | flops 3627810816 | bytes 12589056 | tf_op jit(solution)/shard_map/dot_general | solution.py:22
  199.7 8.4 %shard_map.277 = (f32[192,1536]{1,0:T(8,128)}, f32[192,1536]{1,0:T(8,128)}, f32[192,1536]{1,0:T(8,128)}, f32[192,1536]{1,0:T(8,128)}) custom-call(s32[2]{0:T(128)} %pad_add_fusion.place, f32[512,768]{1,0:T(8,128)} %copy-done.12, f32[512,1536]{1,0:T(8,128)} %get-tuple-element.192.refs_1_), custom_call_target="tpu_custom_call" | custom-call | tf_op jit(solution)/shard_map/pallas_call | solution.py:331
  212.0 8.0 %fusion.46 = (f32[1536]{0:T(1024)S(1)}, f32[512,1536]{1,0:T(8,128)}) fusion(f32[512,1536]{1,0:T(8,128)S(1)} %get-tuple-element.193, f32[512,768]{1,0:T(8,128)S(1)} %copy-done.13, f32[768,1536]{1,0:T(8,128)} %shard_map.273), kind=kOutput, calls=%fused_computation.176 | convolution fusion | flops 3631741440 | bytes 12589056 | tf_op jit(solution)/shard_map/dot_general | solution.py:22
  225.6 9.9 %shard_map.275 = (f32[192,1920]{1,0:T(8,128)}, f32[192,1920]{1,0:T(8,128)}, f32[192,1920]{1,0:T(8,128)}, f32[192,1920]{1,0:T(8,128)}) custom-call(s32[2]{0:T(128)} %pad_add_fusion.place, f32[512,768]{1,0:T(8,128)} %copy-done.17, f32[512,1536]{1,0:T(8,128)} %get-tuple-element.195.refs_1_), custom_call_target="tpu_custom_call" | custom-call | tf_op jit(solution)/shard_map/pallas_call | solution.py:331
  235.5 7.5 %fusion.49 = f32[512,768]{1,0:T(8,128)} fusion(f32[512,1536]{1,0:T(8,128)S(1)} %copy-done.2, f32[768,1536]{1,0:T(8,128)} %get-tuple-element.57), kind=kOutput, calls=%fused_computation.179 | convolution fusion | flops 3623878656 | bytes 9437184 | tf_op jit(solution)/shard_map/dot_general | solution.py:22
  248.4 11.7 %collective-permute-done.38 = f32[96,1536]{1,0:T(8,128)S(1)} collective-permute-done((f32[96,1536]{1,0:T(8,128)}, f32[96,1536]{1,0:T(8,128)S(1)}, u32[]{:S(2)}, u32[]{:S(2)}) %collective-permute-start.38) | collective-permute-done | bytes 589856 | tf_op jit(solution)/shard_map/ppermute | solution.py:206
  268.7 10.6 %aq.1 = f32[2,256,384]{2,1,0:T(8,128)} custom-call(f32[2,656,1152]{2,1,0:T(8,128)} %bitcast.75, f32[2,656,1152]{2,1,0:T(8,128)} %bitcast.76, f32[2,656,1152]{2,1,0:T(8,128)} %bitcast.77, f32[2,256,384]{2,1,0:T(8,128)} %bitcast.84, f32[2,256,384]{2,1,0:T(8,128)} %get-tuple-element.55.out_ref, f32[2,256,384]{2,1,0:T(8,128)} %get-tuple-element.59.lse_ref, ...), custom_call_target="tpu_custom_call" | custom-call | tf_op jit(solution)/shard_map/aq/pallas_call | solution.py:162
  294.1 5.2 shard_map.276
  307.0 4.8 collective-permute-start.35
  319.4 13.1 %ak.1 = (f32[2,256,384]{2,1,0:T(8,128)}, f32[2,256,384]{2,1,0:T(8,128)}) custom-call(f32[2,656,1152]{2,1,0:T(8,128)} %bitcast.78, f32[2,656,384]{2,1,0:T(8,128)} %pad_maximum_fusion.2.g_ref, f32[2,6,656]{2,1,0:T(8,128)} %get-tuple-element.177.lse_ref, f32[2,6,656]{2,1,0:T(8,128)} %get-tuple-element.176.delta_ref, f32[2,656,1152]{2,1,0:T(8,128)} %bitcast.79, ...), custom_call_target="tpu_custom_call" | custom-call | tf_op jit(solution)/shard_map/ak/pallas_call | solution.py:185
  357.4 8.2 %shard_map.274 = (f32[208,1152]{1,0:T(8,128)}, f32[208,1152]{1,0:T(8,128)}, f32[208,1152]{1,0:T(8,128)}, f32[208,1152]{1,0:T(8,128)}) custom-call(s32[2]{0:T(128)} %pad_add_fusion.place, f32[512,768]{1,0:T(8,128)} %pad_maximum_fusion.3.refs_0_, f32[512,1152]{1,0:T(8,128)} %bitcast.86), custom_call_target="tpu_custom_call" | custom-call | tf_op jit(solution)/shard_map/pallas_call | solution.py:331
  377.8 7.1 %collective-permute-done.29 = f32[104,1152]{1,0:T(8,128)S(1)} collective-permute-done((f32[104,1152]{1,0:T(8,128)}, f32[104,1152]{1,0:T(8,128)S(1)}, u32[]{:S(2)}, u32[]{:S(2)}) %collective-permute-start.29) | collective-permute-done | bytes 479264 | tf_op jit(solution)/shard_map/ppermute | solution.py:206
  395.0 21.6 %collective-permute-done.34 = f32[192,1920]{1,0:T(8,128)} collective-permute-done((f32[192,1920]{1,0:T(8,128)}, f32[192,1920]{1,0:T(8,128)}, u32[]{:S(2)}, u32[]{:S(2)}) %collective-permute-start.34) | collective-permute-done | bytes 1474592 | tf_op jit(solution)/shard_map/ppermute | solution.py:206
  419.0 17.5 %collective-permute-done.28 = f32[208,1152]{1,0:T(8,128)S(1)} collective-permute-done((f32[208,1152]{1,0:T(8,128)S(1)}, f32[208,1152]{1,0:T(8,128)S(1)}, u32[]{:S(2)}, u32[]{:S(2)}) %collective-permute-start.28) | collective-permute-done | bytes 958496 | tf_op jit(solution)/shard_map/ppermute | solution.py:206
  445.1 57.6 %all-reduce.16.cloned.1.call-done = (f32[96,3072]{1,0:T(8,128)}, f32[96,768]{1,0:T(8,128)}) async-done(((f32[96,3072]{1,0:T(8,128)}, f32[96,768]{1,0:T(8,128)}), (f32[96,3072]{1,0:T(8,128)}, f32[96,768]{1,0:T(8,128)})) %all-reduce.16.cloned.1.call-update) | async-done | bytes 1474576 | tf_op jit(solution)/shard_map/psum | solution.py:747
  505.0 49.6 %all-reduce.14.cloned.1.call-done = f32[100,2304]{1,0:T(8,128)} async-done(((f32[100,2304]{1,0:T(8,128)}), f32[100,2304]{1,0:T(8,128)}) %all-reduce.14.cloned.1.call-update) | async-done | bytes 921616 | tf_op jit(solution)/shard_map/psum | solution.py:761
  (412 shorter events, 218.3 us)
Async XLA Ops:
  7.2 430.4 %all-reduce.12.cloned.1.call-start = ((), (), s32[]{:S(2)}) async-start(), calls=%async_computation | async-start | bytes 2359296 | tf_op jit(solution)/shard_map/psum | solution.py:740
  21.5 31.9 %collective-permute-start.3 = (f32[208,1152]{1,0:T(8,128)S(1)}, f32[208,1152]{1,0:T(8,128)S(1)}, u32[]{:S(2)}, u32[]{:S(2)}) collective-permute-start(f32[208,1152]{1,0:T(8,128)S(1)} %pad_maximum_fusion.10.refs_0_), channel_id=1, source_target_pairs={{0,8},{4,12},{8,0},{12,4},{16,24},{20,28},{24,16},{28,20},{1,9},{5... | collective-permute-start | bytes 2875400 | tf_op jit(solution)/shard_map/ppermute | solution.py:206
  27.5 59.6 %collective-permute-start.9 = (f32[192,1920]{1,0:T(8,128)S(1)}, f32[192,1920]{1,0:T(8,128)S(1)}, u32[]{:S(2)}, u32[]{:S(2)}) collective-permute-start(f32[192,1920]{1,0:T(8,128)S(1)} %maximum_maximum_fusion.refs_0_), channel_id=1, source_target_pairs={{0,8},{4,12},{8,0},{12,4},{16,24},{20,28},{24,16},{28,20},{1,9},{5... | collective-permute-start | bytes 4423688 | tf_op jit(solution)/shard_map/ppermute | solution.py:206
  27.7 62.9 %collective-permute-start.10 = (f32[192,1920]{1,0:T(8,128)S(1)}, f32[192,1920]{1,0:T(8,128)S(1)}, u32[]{:S(2)}, u32[]{:S(2)}) collective-permute-start(f32[192,1920]{1,0:T(8,128)S(1)} %maximum_maximum_fusion.refs_0_), channel_id=1, source_target_pairs={{0,16},{4,20},{8,24},{12,28},{16,0},{20,4},{24,8},{28,12},{1,17},{... | collective-permute-start | bytes 4423688 | tf_op jit(solution)/shard_map/ppermute | solution.py:206
  55.2 70.9 %collective-permute-start.4 = (f32[664,768]{1,0:T(8,128)}, f32[664,768]{1,0:T(8,128)}, u32[]{:S(2)}, u32[]{:S(2)}) collective-permute-start(f32[664,768]{1,0:T(8,128)} %select_maximum_fusion), channel_id=1, source_target_pairs={{0,4},{4,0},{8,12},{12,8},{16,20},{20,16},{24,28},{28,24},{1,5},{5... | collective-permute-start | bytes 6119432 | tf_op jit(solution)/shard_map/ppermute | solution.py:206
  55.2 31.0 %collective-permute-start.5 = (f32[208,1152]{1,0:T(8,128)S(1)}, f32[208,1152]{1,0:T(8,128)S(1)}, u32[]{:S(2)}, u32[]{:S(2)}) collective-permute-start(f32[208,1152]{1,0:T(8,128)S(1)} %pad_maximum_fusion.10.refs_0_), channel_id=1, source_target_pairs={{0,16},{4,20},{8,24},{12,28},{16,0},{20,4},{24,8},{28,12},{1,17},{... | collective-permute-start | bytes 2875400 | tf_op jit(solution)/shard_map/ppermute | solution.py:206
  56.5 40.2 %collective-permute-start.6 = (f32[104,1152]{1,0:T(8,128)}, f32[104,1152]{1,0:T(8,128)}, u32[]{:S(2)}, u32[]{:S(2)}) collective-permute-start(f32[104,1152]{1,0:T(8,128)} %slice.453), channel_id=1, source_target_pairs={{0,16},{4,20},{8,24},{12,28},{16,0},{20,4},{24,8},{28,12},{1,17},{... | collective-permute-start | bytes 1437704 | tf_op jit(solution)/shard_map/ppermute | solution.py:206
  114.1 49.0 %collective-permute-start.15 = (f32[192,1536]{1,0:T(8,128)}, f32[192,1536]{1,0:T(8,128)}, u32[]{:S(2)}, u32[]{:S(2)}) collective-permute-start(f32[192,1536]{1,0:T(8,128)} %pad_maximum_fusion.7.refs_0_), channel_id=1, source_target_pairs={{0,8},{4,12},{8,0},{12,4},{16,24},{20,28},{24,16},{28,20},{1,9},{5... | collective-permute-start | bytes 3538952 | tf_op jit(solution)/shard_map/ppermute | solution.py:206
  114.1 51.7 %collective-permute-start.16 = (f32[192,1536]{1,0:T(8,128)}, f32[192,1536]{1,0:T(8,128)}, u32[]{:S(2)}, u32[]{:S(2)}) collective-permute-start(f32[192,1536]{1,0:T(8,128)} %pad_maximum_fusion.7.refs_0_), channel_id=1, source_target_pairs={{0,16},{4,20},{8,24},{12,28},{16,0},{20,4},{24,8},{28,12},{1,17},{... | collective-permute-start | bytes 3538952 | tf_op jit(solution)/shard_map/ppermute | solution.py:206
  124.8 32.4 %collective-permute-start.13 = (f32[2,96,768]{2,1,0:T(8,128)}, f32[2,96,768]{2,1,0:T(8,128)}, u32[]{:S(2)}, u32[]{:S(2)}) collective-permute-start(f32[2,96,768]{2,1,0:T(8,128)} %dynamic-slice_bitcast_fusion.1), channel_id=1, source_target_pairs={{0,4},{4,0},{8,12},{12,8},{16,20},{20,16},{24,28},{28,24},{1,5},{5... | collective-permute-start | bytes 1769480 | tf_op jit(solution)/shard_map/ppermute | solution.py:206
  171.7 117.6 %collective-permute-start.32 = (f32[512,384]{1,0:T(8,128)}, f32[512,384]{1,0:T(8,128)}, u32[]{:S(2)}, u32[]{:S(2)}) collective-permute-start(f32[512,384]{1,0:T(8,128)} %bitcast.9.refs_0_), channel_id=1, source_target_pairs={{0,4},{4,0},{8,12},{12,8},{16,20},{20,16},{24,28},{28,24},{1,5},{5... | collective-permute-start | bytes 2359304 | tf_op jit(solution)/shard_map/ppermute | solution.py:206
  210.6 34.9 %collective-permute-start.40 = (f32[96,1536]{1,0:T(8,128)}, f32[96,1536]{1,0:T(8,128)}, u32[]{:S(2)}, u32[]{:S(2)}) collective-permute-start(f32[96,1536]{1,0:T(8,128)} %get-tuple-element.130), channel_id=1, source_target_pairs={{0,16},{4,20},{8,24},{12,28},{16,0},{20,4},{24,8},{28,12},{1,17},{... | collective-permute-start | bytes 1769480 | tf_op jit(solution)/shard_map/ppermute | solution.py:206
  248.1 53.8 %collective-permute-start.41 = (f32[192,1536]{1,0:T(8,128)}, f32[192,1536]{1,0:T(8,128)}, u32[]{:S(2)}, u32[]{:S(2)}) collective-permute-start(f32[192,1536]{1,0:T(8,128)} %pad_maximum_fusion.9), channel_id=1, source_target_pairs={{0,8},{4,12},{8,0},{12,4},{16,24},{20,28},{24,16},{28,20},{1,9},{5... | collective-permute-start | bytes 3538952 | tf_op jit(solution)/shard_map/ppermute | solution.py:206
  261.4 40.6 %collective-permute-start.39 = (f32[192,1536]{1,0:T(8,128)}, f32[192,1536]{1,0:T(8,128)}, u32[]{:S(2)}, u32[]{:S(2)}) collective-permute-start(f32[192,1536]{1,0:T(8,128)} %pad_maximum_fusion.8), channel_id=1, source_target_pairs={{0,16},{4,20},{8,24},{12,28},{16,0},{20,4},{24,8},{28,12},{1,17},{... | collective-permute-start | bytes 3538952 | tf_op jit(solution)/shard_map/ppermute | solution.py:206
  302.0 200.8 %collective-permute-start.19 = (f32[256,768]{1,0:T(8,128)}, f32[256,768]{1,0:T(8,128)}, u32[]{:S(2)}, u32[]{:S(2)}) collective-permute-start(f32[256,768]{1,0:T(8,128)} %slice.476), channel_id=1, source_target_pairs={{0,4},{4,0},{8,12},{12,8},{16,20},{20,16},{24,28},{28,24},{1,5},{5... | collective-permute-start | bytes 2359304 | tf_op jit(solution)/shard_map/ppermute | solution.py:206
  307.0 33.2 %collective-permute-start.35 = (f32[96,1920]{1,0:T(8,128)}, f32[96,1920]{1,0:T(8,128)}, u32[]{:S(2)}, u32[]{:S(2)}) collective-permute-start(f32[96,1920]{1,0:T(8,128)} %get-tuple-element.124), channel_id=1, source_target_pairs={{0,16},{4,20},{8,24},{12,28},{16,0},{20,4},{24,8},{28,12},{1,17},{... | collective-permute-start | bytes 2211848 | tf_op jit(solution)/shard_map/ppermute | solution.py:206
  312.8 33.7 %collective-permute-start.33 = (f32[96,1920]{1,0:T(8,128)}, f32[96,1920]{1,0:T(8,128)}, u32[]{:S(2)}, u32[]{:S(2)}) collective-permute-start(f32[96,1920]{1,0:T(8,128)} %get-tuple-element.123), channel_id=1, source_target_pairs={{0,8},{4,12},{8,0},{12,4},{16,24},{20,28},{24,16},{28,20},{1,9},{5... | collective-permute-start | bytes 2211848 | tf_op jit(solution)/shard_map/ppermute | solution.py:206
  315.4 58.7 %collective-permute-start.42 = (f32[96,1536]{1,0:T(8,128)}, f32[96,1536]{1,0:T(8,128)}, u32[]{:S(2)}, u32[]{:S(2)}) collective-permute-start(f32[96,1536]{1,0:T(8,128)} %get-tuple-element.109), channel_id=1, source_target_pairs={{0,4},{4,0},{8,12},{12,8},{16,20},{20,16},{24,28},{28,24},{1,5},{5... | collective-permute-start | bytes 1769480 | tf_op jit(solution)/shard_map/ppermute | solution.py:206
  342.7 52.3 %collective-permute-start.36 = (f32[192,1920]{1,0:T(8,128)}, f32[192,1920]{1,0:T(8,128)}, u32[]{:S(2)}, u32[]{:S(2)}) collective-permute-start(f32[192,1920]{1,0:T(8,128)} %pad_maximum_fusion.5), channel_id=1, source_target_pairs={{0,8},{4,12},{8,0},{12,4},{16,24},{20,28},{24,16},{28,20},{1,9},{5... | collective-permute-start | bytes 4423688 | tf_op jit(solution)/shard_map/ppermute | solution.py:206
  374.1 42.5 %collective-permute-start.34 = (f32[192,1920]{1,0:T(8,128)}, f32[192,1920]{1,0:T(8,128)}, u32[]{:S(2)}, u32[]{:S(2)}) collective-permute-start(f32[192,1920]{1,0:T(8,128)} %pad_maximum_fusion.4), channel_id=1, source_target_pairs={{0,16},{4,20},{8,24},{12,28},{16,0},{20,4},{24,8},{28,12},{1,17},{... | collective-permute-start | bytes 4423688 | tf_op jit(solution)/shard_map/ppermute | solution.py:206
  376.3 126.4 %all-reduce.16.cloned.1.call-start = ((), (), s32[]{:S(2)}) async-start(), calls=%async_computation.2 | async-start | bytes 2949120 | tf_op jit(solution)/shard_map/psum | solution.py:747
  385.0 33.9 %collective-permute-start.30 = (f32[208,1152]{1,0:T(8,128)S(1)}, f32[208,1152]{1,0:T(8,128)S(1)}, u32[]{:S(2)}, u32[]{:S(2)}) collective-permute-start(f32[208,1152]{1,0:T(8,128)S(1)} %pad_maximum_fusion.12), channel_id=1, source_target_pairs={{0,8},{4,12},{8,0},{12,4},{16,24},{20,28},{24,16},{28,20},{1,9},{5... | collective-permute-start | bytes 2875400 | tf_op jit(solution)/shard_map/ppermute | solution.py:206
  390.4 46.0 %collective-permute-start.28 = (f32[208,1152]{1,0:T(8,128)S(1)}, f32[208,1152]{1,0:T(8,128)S(1)}, u32[]{:S(2)}, u32[]{:S(2)}) collective-permute-start(f32[208,1152]{1,0:T(8,128)S(1)} %pad_maximum_fusion.11), channel_id=1, source_target_pairs={{0,16},{4,20},{8,24},{12,28},{16,0},{20,4},{24,8},{28,12},{1,17},{... | collective-permute-start | bytes 2875400 | tf_op jit(solution)/shard_map/ppermute | solution.py:206
  438.7 115.9 %all-reduce.14.cloned.1.call-start = ((), (), s32[]{:S(2)}) async-start(), calls=%async_computation.1 | async-start | bytes 1916928 | tf_op jit(solution)/shard_map/psum | solution.py:761
  (94 other events, 1056.1 us)
Sparse Core Ops, SparseCore 0:
  376.4 54.4 all-reduce.11
  438.8 63.8 all-reduce.15
  505.7 48.8 all-reduce.13
